TPU v7x, 32 devices: a whole 2x2x4 slice. The times are simulated.
32 devices in a mesh: wide: 8 (over z, y), narrow: 4 (over x, core).
Axes of the slice: x: 2, y: 2, z: 4, core: 2. Of those that a mesh axis runs over, the one named last changes fastest.
Arguments:
- amplitudes: float32 [8, 512, 1024], P('wide', None, 'narrow'), may hold values from -6 to 6
- partner: float32 [64, 2048, 1024], P(None, 'wide', 'narrow'), may hold values from -0.1875 to 0.1875
- gate_block: float32 [8, 8], replicated, may hold values from -2 to 2
- slice_bits: int32 [6], replicated, may hold values from 0 to 1, as said below
- bit_order: int32 [9], replicated, may hold values from 0 to 8, each once
Outputs:
- contracted: float32 [8, 512, 2048], P(None, 'wide', 'narrow')
Inputs may be any that keep to these rules, and one draw needn't show every extreme that they name: bit_order is a permutation of 0 to 8. `slice_bits`: each entry is 0 or 1; the bits are never all equal.
All inputs are finite; a program needn't handle non-finite values.
Results may differ from a plain program's by a relative error of at most 0.00007.
Values sent between devices are 32-bit elements; how exact they have to be, the bound alone decides.
A program may use at most 64 MiB of HBM per device.

v0:
```python
import jax
import jax.numpy as jnp
from jax import lax
from jax.sharding import PartitionSpec as P


def source_rows(bit_order, total_rows):
    width = bit_order.shape[0]
    row_ids = jnp.arange(total_rows, dtype=jnp.int32)
    picked = jnp.bitwise_and(jnp.right_shift(row_ids[:, None], bit_order[None, :]), 1)
    powers = jnp.left_shift(jnp.ones((width,), jnp.int32), jnp.arange(width, dtype=jnp.int32))
    return jnp.sum(picked * powers[None, :], axis=1)


def slice_number(slice_bits):
    width = slice_bits.shape[0]
    powers = jnp.left_shift(jnp.ones((width,), jnp.int32), jnp.arange(width, dtype=jnp.int32))
    return jnp.sum(slice_bits * powers)


def contract_partner(left_rows, chosen):
    partial_terms = lax.dot_general(
        left_rows,
        lax.all_gather(chosen, "wide", axis=0, tiled=True),
        (((1,), (1,)), ((), ())),
        precision=lax.Precision.HIGHEST,
        preferred_element_type=jnp.float32,
    )
    return lax.psum_scatter(partial_terms, "narrow", scatter_dimension=1, tiled=True)


def gate_apply(gate_block, received):
    return jnp.einsum("qh,hlc->qlc", gate_block, received, precision=lax.Precision.HIGHEST)


def per_device(amplitudes, partner, gate_block, slice_bits, bit_order):
    source = source_rows(bit_order, amplitudes.shape[1])
    reordered = jnp.take(amplitudes[0], source, axis=0)
    chosen = lax.dynamic_index_in_dim(partner, slice_number(slice_bits), 0, keepdims=False)
    mixed = gate_apply(
        gate_block, lax.all_to_all(reordered[None], "wide", split_axis=1, concat_axis=0, tiled=True)
    )
    out_bits = mixed.shape[0]
    local_rows = mixed.shape[1]
    owned_part = contract_partner(mixed.reshape(out_bits * local_rows, mixed.shape[2]), chosen)
    return owned_part.reshape(out_bits, local_rows, owned_part.shape[1])


def solution(mesh):
    placed = (P("wide", None, "narrow"), P(None, "wide", "narrow"), P(), P(), P())
    return jax.shard_map(
        per_device, mesh=mesh, in_specs=placed, out_specs=P(None, "wide", "narrow"), check_vma=False
    )
```

profile of v0, /device:TPU:1, one launch (start us, length us, event | category | flops | bytes accessed | tf_op | source)
XLA Modules:
  0.0 127.2 jit_solution(4080367930417074534)
XLA Ops:
  6.5 0.0 copy-start
  6.5 0.0 all-gather.3.cloned.1.call-start
  6.5 1.4 %multiply_reduce_fusion.1 = s32[]{:T(128)} fusion(s32[6]{0:T(128)} %param.8), kind=kLoop, calls=%fused_computation.12 | loop fusion | flops 17 | bytes 28 | tf_op jit(solution)/shard_map/reduce_sum | solution.py:18
  9.8 1.7 %constant_dynamic-slice_fusion = f32[1,256,256]{2,1,0:T(8,128)} fusion(f32[64,256,256]{2,1,0:T(8,128)} %param.6, s32[]{:T(128)S(6)} %select_n.34), kind=kLoop, calls=%fused_computation.14 | loop fusion | bytes 524292 | tf_op jit(solution)/shard_map/jit(dynamic_index_in_dim)/dynamic_slice | solution.py:39
  11.5 0.0 all-gather.3.cloned.1.call-update
  11.5 0.0 reduce-scatter.2.cloned.1.call-start
  11.6 0.7 multiply_reduce_fusion
  12.4 0.0 copy-done
  12.4 0.0 copy-start.1
  12.4 1.6 %gather_fusion = f32[512,256]{1,0:T(8,128)S(1)} fusion(f32[512,256]{1,0:T(8,128)S(1)} %bitcast.17, s32[1024]{0:T(1024)S(1)} %pad_clamp_fusion), kind=kCustom, calls=%fused_computation | custom fusion | bytes 1050624 | tf_op jit(solution)/shard_map/jit(_take)/gather | solution.py:38
  14.0 0.1 bitcast_select_fusion
  14.1 0.5 copy.11
  14.7 27.6 %all_to_all.12 = f32[1,512,256]{2,0,1:T(1,128)S(1)} all-to-all(f32[1,512,256]{2,0,1:T(1,128)S(1)} %copy.11), channel_id=1, replica_groups=mesh['wide'=8,'narrow'=4] {'wide'}, dimensions={1} | all-to-all | bytes 1048576 | tf_op jit(solution)/shard_map/all_to_all | solution.py:41
  42.3 0.0 copy-done.1
  42.3 0.9 convolution_bitcast_fusion
  43.2 0.2 copy.13
  43.4 26.0 %all-gather.3.cloned.1.call-done = f32[1,2048,256]{2,1,0:T(8,128)} async-done(((f32[1,256,256]{2,1,0:T(8,128)}), f32[1,2048,256]{2,1,0:T(8,128)}) %all-gather.3.cloned.1.call-update) | async-done | bytes 2097168 | tf_op jit(solution)/shard_map/all_gather | solution.py:24
  69.4 6.7 %fusion = f32[512,2048]{1,0:T(8,128)} fusion(f32[512,256]{1,0:T(8,128)S(1)} %bitcast.19, f32[1,2048,256]{2,1,0:T(8,128)} %all-gather.3.cloned.1.call-done), kind=kOutput, calls=%fused_computation.1 | convolution fusion | flops 3221225472 | bytes 6815744 | tf_op jit(solution)/shard_map/dot_general | solution.py:22
  76.1 0.0 reduce-scatter.2.cloned.1.call-update
  76.1 44.3 %reduce-scatter.2.cloned.1.call-done = f32[512,512]{1,0:T(8,128)} async-done(((f32[512,2048]{1,0:T(8,128)}), f32[512,512]{1,0:T(8,128)}) %reduce-scatter.2.cloned.1.call-update) | async-done | bytes 1048592 | tf_op jit(solution)/shard_map/reduce_scatter | solution.py:29
  (5 shorter events, 0.1 us)
Async XLA Ops:
  6.5 5.8 %copy-start = (f32[1,512,256]{2,1,0:T(8,128)S(1)}, f32[1,512,256]{2,1,0:T(8,128)}, u32[]{:S(2)}) copy-start(f32[1,512,256]{2,1,0:T(8,128)} %param.5) | copy-start | bytes 1572868
  6.5 62.8 %all-gather.3.cloned.1.call-start = ((), (), s32[]{:S(2)}) async-start(), calls=%async_computation.3 | async-start | bytes 2359296 | tf_op jit(solution)/shard_map/all_gather | solution.py:24
  11.5 108.9 %reduce-scatter.2.cloned.1.call-start = ((), (), s32[]{:S(2)}) async-start(), calls=%async_computation.2 | async-start | bytes 5242880 | tf_op jit(solution)/shard_map/reduce_scatter | solution.py:29
  12.4 29.9 %copy-start.1 = (f32[8,8]{1,0:T(8,128)S(1)}, f32[8,8]{1,0:T(8,128)}, u32[]{:S(2)}) copy-start(f32[8,8]{1,0:T(8,128)} %param.7) | copy-start | bytes 772
Sparse Core Ops, SparseCore 0:
  11.7 57.6 all-gather.2
  76.2 44.1 reduce-scatter.1
where the time goes:
time: 128 us; the launch traced here: 127 us
  waiting for transfers between devices  70.3 us (55%)
  blocking collectives  27.6 us (22%)
  between operations  15.4 us (12%)
  matrix products  7.63 us (6%)
  local copies, waits for them, and re-layouts  4 us (3%)
  other arithmetic  2.26 us (2%)
    reduce_scatter x1, waiting for transfers between devices, contract_partner(): lax.psum_scatter(partial_terms, 'narrow', scatter_dimension=1, tiled=True)  44.3 us
    all_to_all x1, blocking collectives, per_device(): lax.all_to_all(reordered[None], 'wide', split_axis=1, concat_axis=0, tile...  27.6 us
    all_gather x1, waiting for transfers between devices, contract_partner(): lax.all_gather(chosen, 'wide', axis=0, tiled=True)  26 us
    dot_general x1, matrix products, contract_partner(): lax.dot_general(left_rows, lax.all_gather(chosen, 'wide', axis=0, tiled=T...  6.75 us
  transfers between devices with their start and end apart: 2, of which 2 were waited for; matrix products, arithmetic and copies ran while one was open for 3% of the time, Pallas kernels for 0%

commit v1 on v0

v1 whole, which is shorter than its diff:
```python
import functools

import jax
import jax.numpy as jnp
from jax import lax
from jax.experimental import pallas as pl
from jax.experimental.pallas import tpu as pltpu
from jax.sharding import PartitionSpec as P

F32 = jnp.float32
BF16 = jnp.bfloat16


def slice_kernel(bits_ref, partner_ref, chosen_ref):
    chosen_ref[...] = partner_ref[0]


def slice_at(bits_ref):
    number = bits_ref[0]
    for j in range(1, bits_ref.shape[0]):
        number = number + bits_ref[j] * (1 << j)
    return number


def choose(partner, slice_bits):
    _, rows, cols = partner.shape
    return pl.pallas_call(
        slice_kernel,
        out_shape=jax.ShapeDtypeStruct((rows, cols), F32),
        grid_spec=pltpu.PrefetchScalarGridSpec(
            num_scalar_prefetch=1,
            grid=(1,),
            in_specs=[pl.BlockSpec((1, rows, cols), lambda i, bits: (slice_at(bits), 0, 0))],
            out_specs=pl.BlockSpec((rows, cols), lambda i, bits: (0, 0)),
        ),
    )(slice_bits, partner)


def split2(x):
    hi = x.astype(BF16)
    return hi, (x - hi.astype(F32)).astype(BF16)


def dot_nt(a, b):
    return lax.dot_general(a, b, (((1,), (1,)), ((), ())), preferred_element_type=F32)


def kernel(wides, order_ref, gate_ref, amp_ref, chosen_ref, out_ref,
           send_a, recv_a, mixed, mix_hi, mix_lo, held, far_part, near_part,
           core_far, core_near, x_in,
           a_send, a_recv, up_send, down_send, z_recv, y_send, y_recv, rs_send, rs_recv):
    me = lax.axis_index("wide")
    nar = lax.axis_index("narrow")
    lines = wides // 2
    group = wides // 4
    zs_per = lines // 4
    z, y = me // 2, me % 2
    x, c = nar // 2, nar % 2
    core_peer = (me, x * 2 + 1 - c)
    x_peer = (me, (1 - x) * 2 + c)
    y_peer = (z * 2 + 1 - y, nar)
    rows, cols = amp_ref.shape
    out_bits, low_rows, wide_cols = out_ref.shape

    def rc(src, dst, ssem, rsem, dev):
        return pltpu.make_async_remote_copy(
            src_ref=src, dst_ref=dst, send_sem=ssem, recv_sem=rsem,
            device_id=dev, device_id_type=pl.DeviceIdType.MESH)

    barrier = pltpu.get_barrier_semaphore()

    @pl.loop(1, wides)
    def _(s):
        pl.semaphore_signal(barrier, inc=1, device_id=((me + s) % wides, nar),
                            device_id_type=pl.DeviceIdType.MESH)
    for peer in (core_peer, x_peer):
        pl.semaphore_signal(barrier, inc=1, device_id=peer, device_id_type=pl.DeviceIdType.MESH)
    held[me] = chosen_ref[...]
    pl.semaphore_wait(barrier, wides + 1)

    def up(zz):
        slot = held.at[zz * 2 + y]
        return rc(slot, slot, up_send.at[zz], z_recv.at[zz], ((z + 1) % lines * 2 + y, nar))

    def down(zz):
        slot = held.at[zz * 2 + y]
        return rc(slot, slot, down_send.at[zz], z_recv.at[zz], ((z + lines - 1) % lines * 2 + y, nar))

    def across(zz):
        slot = held.at[zz * 2 + y]
        return rc(slot, slot, y_send.at[zz], y_recv.at[zz], y_peer)

    def across_in(zz):
        slot = held.at[zz * 2 + 1 - y]
        return rc(slot, slot, y_send.at[zz], y_recv.at[zz], y_peer)

    @pl.when(z < lines - 1)
    def _():
        up(z).start()

    @pl.when(z > 0)
    def _():
        down(z).start()
    across(z).start()

    row_ids = lax.broadcasted_iota(jnp.int32, (rows, 128), 0)
    source = jnp.zeros((rows, 128), jnp.int32)
    for j in range(order_ref.shape[0]):
        source = source + (lax.shift_right_logical(row_ids, jnp.broadcast_to(order_ref[j], row_ids.shape)) & 1) * (1 << j)
    lane = lax.broadcasted_iota(jnp.int32, (rows, 128), 1)
    onehot = jnp.concatenate(
        [jnp.where(lane + t * 128 == source, 1.0, 0.0).astype(BF16) for t in range(rows // 128)], axis=1)
    amp = amp_ref[...]
    a1 = amp.astype(BF16)
    rest = amp - a1.astype(F32)
    a2 = rest.astype(BF16)
    a3 = (rest - a2.astype(F32)).astype(BF16)
    moved = (jnp.dot(onehot, a3, preferred_element_type=F32)
             + jnp.dot(onehot, a2, preferred_element_type=F32)
             + jnp.dot(onehot, a1, preferred_element_type=F32))
    send_a[...] = moved.reshape(send_a.shape)

    def a_out(to):
        return rc(send_a.at[to], recv_a.at[me], a_send.at[to], a_recv.at[me], (to, nar))

    def a_in(frm):
        return rc(send_a.at[frm], recv_a.at[frm], a_send.at[frm], a_recv.at[frm], (frm, nar))

    @pl.loop(1, wides)
    def _(s):
        a_out((me + s) % wides).start()
    recv_a[me] = send_a[me]

    def line_step(d):
        @pl.when(z - d >= 0)
        def _():
            up(z - d).wait_recv()

            @pl.when(z < lines - 1)
            def _():
                up(z - d).start()
            across(z - d).start()

        @pl.when(z + d < lines)
        def _():
            down(z + d).wait_recv()

            @pl.when(z > 0)
            def _():
                down(z + d).start()
            across(z + d).start()

    line_step(1)

    @pl.loop(1, wides)
    def _(s):
        a_in((me + s) % wides).wait_recv()

    @pl.loop(0, out_bits)
    def _(q):
        acc = gate_ref[q, 0] * recv_a[0]
        for h in range(1, wides):
            acc = acc + gate_ref[q, h] * recv_a[h]
        mixed[q] = acc
    hi, lo = split2(mixed[...].reshape(rows, cols))
    mix_hi[...] = hi
    mix_lo[...] = lo

    def product(o, dst, role):
        @pl.loop(0, zs_per)
        def _(i):
            across_in(o * zs_per + i).wait_recv()
        b = held[pl.ds(o * group, group)].reshape(wide_cols, cols)
        bh, bl = split2(b)
        mh, ml = mix_hi[...], mix_lo[...]
        dst[role] = dot_nt(mh, bl) + dot_nt(ml, bh) + dot_nt(mh, bh)

    def core_send(src, dst, k):
        return rc(src, dst, rs_send.at[k], rs_recv.at[k], core_peer)

    far_core = core_send(far_part.at[1], core_far, 0)
    near_core = core_send(near_part.at[1], core_near, 1)
    over_x = rc(far_part.at[0], x_in, rs_send.at[2], rs_recv.at[2], x_peer)

    def remote_chunk(o):
        role = (o + c) % 2
        product(o, far_part, role)

        @pl.when(role == 1)
        def _():
            far_core.start()

        @pl.when(role == 0)
        def _():
            far_core.wait_recv()
            far_part[0] = far_part[0] + core_far[...]
            over_x.start()

    def local_chunk(o):
        role = (o + c) % 2
        product(o, near_part, role)

        @pl.when(role == 1)
        def _():
            near_core.start()

    here = z // zs_per
    remote_low = (1 - x) * 2
    first = jnp.where(here > remote_low, remote_low + 1, remote_low)
    second = remote_low * 2 + 1 - first
    last_near = 3 * zs_per - 1
    for d in range(2, last_near + 1):
        line_step(d)
    remote_chunk(first)
    for d in range(max(2, last_near + 1), lines):
        line_step(d)
    remote_chunk(second)
    local_chunk(x * 2 + 1 - c)
    local_chunk(nar)
    near_core.wait_recv()
    near_part[0] = near_part[0] + core_near[...]
    over_x.wait_recv()
    out_ref[...] = (near_part[0] + x_in[...]).reshape(out_ref.shape)

    far_core.wait_send()
    near_core.wait_send()
    over_x.wait_send()

    @pl.loop(1, wides)
    def _(s):
        a_out((me + s) % wides).wait_send()
    for zz in range(lines):
        across(zz).wait_send()

        @pl.when((z < lines - 1) & (zz <= z))
        def _():
            up(zz).wait_send()

        @pl.when((z > 0) & (zz >= z))
        def _():
            down(zz).wait_send()


def solution(mesh):
    wides = mesh.shape["wide"]

    def per_device(amplitudes, partner, gate_block, slice_bits, bit_order):
        chosen = choose(partner, slice_bits)
        rows, cols = amplitudes.shape[1:]
        out_bits = gate_block.shape[0]
        low_rows = rows // wides
        block = chosen.shape[0]
        total = block * wides
        own = total // mesh.shape["narrow"]
        flat = out_bits * low_rows
        smem = pl.BlockSpec(memory_space=pltpu.SMEM)
        vmem = pl.BlockSpec(memory_space=pltpu.VMEM)
        dma = pltpu.SemaphoreType.DMA
        lines = wides // 2
        return pl.pallas_call(
            functools.partial(kernel, wides),
            out_shape=jax.ShapeDtypeStruct((out_bits, low_rows, own), F32),
            in_specs=[smem, smem, vmem, vmem],
            out_specs=vmem,
            scratch_shapes=[
                pltpu.VMEM((wides, low_rows, cols), F32),
                pltpu.VMEM((wides, low_rows, cols), F32),
                pltpu.VMEM((out_bits, low_rows, cols), F32),
                pltpu.VMEM((flat, cols), BF16),
                pltpu.VMEM((flat, cols), BF16),
                pltpu.VMEM((wides, block, cols), F32),
                pltpu.VMEM((2, flat, own), F32),
                pltpu.VMEM((2, flat, own), F32),
                pltpu.VMEM((flat, own), F32),
                pltpu.VMEM((flat, own), F32),
                pltpu.VMEM((flat, own), F32),
                dma((wides,)), dma((wides,)),
                dma((lines,)), dma((lines,)), dma((lines,)), dma((lines,)), dma((lines,)),
                dma((3,)), dma((3,)),
            ],
            compiler_params=pltpu.CompilerParams(
                collective_id=0, has_side_effects=True, vmem_limit_bytes=48 * 1024 * 1024),
        )(bit_order, gate_block, amplitudes[0], chosen)

    placed = (P("wide", None, "narrow"), P(None, "wide", "narrow"), P(), P(), P())
    return jax.shard_map(
        per_device, mesh=mesh, in_specs=placed, out_specs=P(None, "wide", "narrow"), check_vma=False
    )
```

time: 128 us -> 63.2 us (0.49)
  waiting for transfers between devices: 70.3 us -> 0 us
  Pallas kernels: 0 us -> 61 us
  blocking collectives: 27.6 us -> 0 us
  between operations: 15.4 us -> 0.03 us
  matrix products: 7.63 us -> 0 us
  other arithmetic: 2.26 us -> 0 us
  local copies, waits for them, and re-layouts: 4 us -> 1.93 us
    pallas_call x0 -> x2, Pallas kernels: none -> 61 us  [the longest x1 58.5 us: per_device(): pl.pallas_call(functools.partial(kernel, wides), out_shape=jax.ShapeDtype...]
    reduce_scatter x1 -> x0, waiting for transfers between devices: 44.3 us -> none  [contract_partner(): lax.psum_scatter(partial_terms, 'narrow', scatter_dimension=1, tiled=True)]
    all_to_all x1 -> x0, blocking collectives: 27.6 us -> none  [per_device(): lax.all_to_all(reordered[None], 'wide', split_axis=1, concat_axis=0, tile...]
    all_gather x1 -> x0, waiting for transfers between devices: 26 us -> none  [contract_partner(): lax.all_gather(chosen, 'wide', axis=0, tiled=True)]
    dot_general x2 -> x0, matrix products: 7.63 us -> none  [the longest x1 6.75 us: contract_partner(): lax.dot_general(left_rows, lax.all_gather(chosen, 'wide', axis=0, tiled=T...]
    reduce_sum x2 -> x0, other arithmetic: 2.1 us -> none  [the longest x1 1.35 us: slice_number(): return jnp.sum(slice_bits * powers)]
    unnamed x5 -> x9, local copies, waits for them, and re-layouts: 0.05 us -> 1.93 us
    dynamic_slice x1 -> x0, local copies, waits for them, and re-layouts: 1.67 us -> none  [per_device(): lax.dynamic_index_in_dim(partner, slice_number(slice_bits), 0, keepdims=F...]
  transfers between devices with their start and end apart: 2 -> 0, of which waited for: 2 -> 0; matrix products, arithmetic and copies ran while one was open for 3% -> 0% of each run, Pallas kernels for 0% -> 0%
where the time goes in v1:
time: 63.2 us; the launch traced here: 62.9 us
  Pallas kernels  61 us (97%)
  local copies, waits for them, and re-layouts  1.93 us (3%)
    pallas_call x1, Pallas kernels, per_device(): pl.pallas_call(functools.partial(kernel, wides), out_shape=jax.ShapeDtype...  58.5 us
    pallas_call x1, Pallas kernels, choose(): pl.pallas_call(slice_kernel, out_shape=jax.ShapeDtypeStruct((rows, cols),...  2.47 us
    unnamed x9, local copies, waits for them, and re-layouts  1.93 us

profile of v1, /device:TPU:1, one launch (start us, length us, event | category | flops | bytes accessed | tf_op | source)
XLA Modules:
  0.0 62.9 jit_solution(10069135091381937112)
XLA Ops:
  0.0 0.0 copy-start.3
  0.0 0.0 copy-start.2
  0.0 0.0 copy-start.1
  0.0 2.5 %shard_map.55.chosen_ref = f32[256,256]{1,0:T(8,128)} custom-call(s32[6]{0:T(128)} %bits_ref.1, f32[64,256,256]{2,1,0:T(8,128)} %partner_ref.1), custom_call_target="tpu_custom_call" | custom-call | tf_op jit(solution)/shard_map/pallas_call | solution.py:27
  2.5 0.0 copy-done.3
  2.5 0.0 copy-done.2
  2.5 0.0 copy-done.1
  2.5 0.0 copy-start
  2.5 0.9 %copy-done = f32[256,256]{1,0:T(8,128)S(1)} copy-done((f32[256,256]{1,0:T(8,128)S(1)}, f32[256,256]{1,0:T(8,128)}, u32[]{:S(2)}) %copy-start) | copy-done | bytes 262168
  3.4 58.5 %shard_map.56 = f32[8,64,512]{2,1,0:T(8,128)S(1)} custom-call(s32[9]{0:T(128)S(1)} %copy-done.3, f32[8,8]{1,0:T(8,128)S(1)} %copy-done.2, f32[512,256]{1,0:T(8,128)S(1)} %bitcast.1, f32[256,256]{1,0:T(8,128)S(1)} %copy-done), custom_call_target="tpu_custom_call" | custom-call | tf_op jit(solution)/shard_map/pallas_call | solution.py:260
  61.9 1.0 %copy.7 = f32[8,64,512]{2,1,0:T(8,128)} copy(f32[8,64,512]{2,1,0:T(8,128)S(1)} %shard_map.56) | data formatting | bytes 2097152
Async XLA Ops:
  0.0 2.5 %copy-start.3 = (s32[9]{0:T(128)S(1)}, s32[9]{0:T(128)}, u32[]{:S(2)}) copy-start(s32[9]{0:T(128)} %order_ref.1) | copy-start | bytes 112
  0.0 2.5 %copy-start.2 = (f32[8,8]{1,0:T(8,128)S(1)}, f32[8,8]{1,0:T(8,128)}, u32[]{:S(2)}) copy-start(f32[8,8]{1,0:T(8,128)} %gate_ref.1) | copy-start | bytes 772
  0.0 2.5 %copy-start.1 = (f32[1,512,256]{2,1,0:T(8,128)S(1)}, f32[1,512,256]{2,1,0:T(8,128)}, u32[]{:S(2)}) copy-start(f32[1,512,256]{2,1,0:T(8,128)} %param.5) | copy-start | bytes 1572868
  2.5 1.0 %copy-start = (f32[256,256]{1,0:T(8,128)S(1)}, f32[256,256]{1,0:T(8,128)}, u32[]{:S(2)}) copy-start(f32[256,256]{1,0:T(8,128)} %shard_map.55.chosen_ref) | copy-start | bytes 786436

commit v2 on v1

v2 whole, which is shorter than its diff:
```python
import functools

import jax
import jax.numpy as jnp
from jax import lax
from jax.experimental import pallas as pl
from jax.experimental.pallas import tpu as pltpu
from jax.sharding import PartitionSpec as P

F32 = jnp.float32
BF16 = jnp.bfloat16


def slice_kernel(bits_ref, partner_ref, chosen_ref, sem):
    number = bits_ref[0]
    for j in range(1, bits_ref.shape[0]):
        number = number + bits_ref[j] * (1 << j)
    copy = pltpu.make_async_copy(partner_ref.at[number], chosen_ref, sem)
    copy.start()
    copy.wait()


def choose(partner, slice_bits):
    _, rows, cols = partner.shape
    return pl.pallas_call(
        slice_kernel,
        out_shape=jax.ShapeDtypeStruct((rows, cols), F32),
        in_specs=[pl.BlockSpec(memory_space=pltpu.SMEM), pl.BlockSpec(memory_space=pl.ANY)],
        out_specs=pl.BlockSpec(memory_space=pltpu.VMEM),
        scratch_shapes=[pltpu.SemaphoreType.DMA],
    )(slice_bits, partner)


def split2(x):
    hi = x.astype(BF16)
    return hi, (x - hi.astype(F32)).astype(BF16)


def dot_nt(a, b):
    return lax.dot_general(a, b, (((1,), (1,)), ((), ())), preferred_element_type=F32)


PIECES = 4
HALVES = 2


def kernel(wides, order_ref, gate_ref, amp_hbm, chosen_ref, out_ref,
           amp_ref, send_a, recv_a, mixed, mix_hi, mix_lo, held, far_part, near_part,
           core_far, core_near, x_in, amp_sem,
           a_send, a_recv, up_send, down_send, z_recv, y_send, y_recv,
           far_send, far_recv, near_send, near_recv, x_send, x_recv):
    me = lax.axis_index("wide")
    nar = lax.axis_index("narrow")
    lines = wides // 2
    group = wides // 4
    zs_per = lines // 4
    z, y = me // 2, me % 2
    x, c = nar // 2, nar % 2
    core_peer = (me, x * 2 + 1 - c)
    x_peer = (me, (1 - x) * 2 + c)
    y_peer = (z * 2 + 1 - y, nar)
    rows, cols = amp_ref.shape
    out_bits, low_rows, wide_cols = out_ref.shape
    half = held.shape[1] // HALVES
    flat = out_bits * low_rows

    def rc(src, dst, ssem, rsem, dev):
        return pltpu.make_async_remote_copy(
            src_ref=src, dst_ref=dst, send_sem=ssem, recv_sem=rsem,
            device_id=dev, device_id_type=pl.DeviceIdType.MESH)

    barrier = pltpu.get_barrier_semaphore()
    amp_copy = pltpu.make_async_copy(amp_hbm, amp_ref, amp_sem)
    amp_copy.start()

    @pl.loop(1, wides)
    def _(s):
        pl.semaphore_signal(barrier, inc=1, device_id=((me + s) % wides, nar),
                            device_id_type=pl.DeviceIdType.MESH)
    for peer in (core_peer, x_peer):
        pl.semaphore_signal(barrier, inc=1, device_id=peer, device_id_type=pl.DeviceIdType.MESH)
    held[me] = chosen_ref[...]

    row_ids = lax.broadcasted_iota(jnp.int32, (rows, 128), 0)
    source = jnp.zeros((rows, 128), jnp.int32)
    for j in range(order_ref.shape[0]):
        source = source + (lax.shift_right_logical(row_ids, jnp.broadcast_to(order_ref[j], row_ids.shape)) & 1) * (1 << j)
    lane = lax.broadcasted_iota(jnp.int32, (rows, 128), 1)
    onehot = jnp.concatenate(
        [jnp.where(lane + t * 128 == source, 1.0, 0.0).astype(BF16) for t in range(rows // 128)], axis=1)
    amp_copy.wait()
    amp = amp_ref[...]
    a1 = amp.astype(BF16)
    rest = amp - a1.astype(F32)
    a2 = rest.astype(BF16)
    a3 = (rest - a2.astype(F32)).astype(BF16)
    moved = (jnp.dot(onehot, a3, preferred_element_type=F32)
             + jnp.dot(onehot, a2, preferred_element_type=F32)
             + jnp.dot(onehot, a1, preferred_element_type=F32))
    send_a[...] = moved.reshape(send_a.shape)
    pl.semaphore_wait(barrier, wides + 1)

    def slot(w, p):
        return held.at[w, pl.ds(p * half, half)]

    def up(zz, p):
        block = slot(zz * 2 + y, p)
        return rc(block, block, up_send.at[zz, p], z_recv.at[zz, p], ((z + 1) % lines * 2 + y, nar))

    def down(zz, p):
        block = slot(zz * 2 + y, p)
        return rc(block, block, down_send.at[zz, p], z_recv.at[zz, p], ((z + lines - 1) % lines * 2 + y, nar))

    def across(zz, p):
        block = slot(zz * 2 + y, p)
        return rc(block, block, y_send.at[zz, p], y_recv.at[zz, p], y_peer)

    def across_in(zz, p):
        block = slot(zz * 2 + 1 - y, p)
        return rc(block, block, y_send.at[zz, p], y_recv.at[zz, p], y_peer)

    for p in range(HALVES):
        @pl.when(z < lines - 1)
        def _():
            up(z, p).start()

        @pl.when(z > 0)
        def _():
            down(z, p).start()
        across(z, p).start()

    def a_out(to):
        return rc(send_a.at[to], recv_a.at[me], a_send.at[to], a_recv.at[me], (to, nar))

    def a_in(frm):
        return rc(send_a.at[frm], recv_a.at[frm], a_send.at[frm], a_recv.at[frm], (frm, nar))

    @pl.loop(1, wides)
    def _(s):
        a_out((me + s) % wides).start()
    recv_a[me] = send_a[me]

    def line_step(d):
        for p in range(HALVES):
            @pl.when(z - d >= 0)
            def _():
                up(z - d, p).wait_recv()

                @pl.when(z < lines - 1)
                def _():
                    up(z - d, p).start()
                across(z - d, p).start()

            @pl.when(z + d < lines)
            def _():
                down(z + d, p).wait_recv()

                @pl.when(z > 0)
                def _():
                    down(z + d, p).start()
                across(z + d, p).start()

    def product(o, dst, role):
        @pl.loop(0, zs_per)
        def _(i):
            for p in range(HALVES):
                across_in(o * zs_per + i, p).wait_recv()
        b = held[pl.ds(o * group, group)].reshape(wide_cols, cols)
        bh, bl = split2(b)
        mh, ml = mix_hi[...], mix_lo[...]
        dst[role] = dot_nt(mh, bl) + dot_nt(ml, bh) + dot_nt(mh, bh)

    piece = flat // PIECES

    def part(p):
        return pl.ds(p * piece, piece)

    def far_core(p):
        return rc(far_part.at[1, part(p)], core_far.at[part(p)], far_send.at[p], far_recv.at[p], core_peer)

    def over_x(p):
        return rc(far_part.at[0, part(p)], x_in.at[part(p)], x_send.at[p], x_recv.at[p], x_peer)

    near_core = rc(near_part.at[1], core_near, near_send, near_recv, core_peer)

    def remote_chunk(o):
        role = (o + c) % 2
        product(o, far_part, role)

        @pl.when(role == 1)
        def _():
            for p in range(PIECES):
                far_core(p).start()

        @pl.when(role == 0)
        def _():
            for p in range(PIECES):
                far_core(p).wait_recv()
                far_part[0, part(p)] = far_part[0, part(p)] + core_far[part(p)]
                over_x(p).start()

    here = z // zs_per
    remote_low = (1 - x) * 2
    first = jnp.where(here > remote_low, remote_low + 1, remote_low)
    second = remote_low * 2 + 1 - first
    last_near = max(3 * zs_per - 1, 1)
    for d in range(1, last_near + 1):
        line_step(d)

    @pl.loop(1, wides)
    def _(s):
        a_in((me + s) % wides).wait_recv()

    @pl.loop(0, out_bits)
    def _(q):
        acc = gate_ref[q, 0] * recv_a[0]
        for h in range(1, wides):
            acc = acc + gate_ref[q, h] * recv_a[h]
        mixed[q] = acc
    hi, lo = split2(mixed[...].reshape(flat, cols))
    mix_hi[...] = hi
    mix_lo[...] = lo

    remote_chunk(first)
    for d in range(last_near + 1, lines):
        line_step(d)
    remote_chunk(second)
    product(x * 2 + 1 - c, near_part, 1)
    near_core.start()
    product(nar, near_part, 0)
    near_core.wait_recv()
    near_part[0] = near_part[0] + core_near[...]
    for p in range(PIECES):
        over_x(p).wait_recv()
        qs = out_bits // PIECES
        out_ref[p * qs:(p + 1) * qs] = (near_part[0, part(p)] + x_in[part(p)]).reshape(qs, low_rows, wide_cols)

    near_core.wait_send()
    for p in range(PIECES):
        far_core(p).wait_send()
        over_x(p).wait_send()

    @pl.loop(1, wides)
    def _(s):
        a_out((me + s) % wides).wait_send()
    for p in range(HALVES):
        @pl.loop(0, lines)
        def _(zz):
            across(zz, p).wait_send()

            @pl.when((z < lines - 1) & (zz <= z))
            def _():
                up(zz, p).wait_send()

            @pl.when((z > 0) & (zz >= z))
            def _():
                down(zz, p).wait_send()


def solution(mesh):
    wides = mesh.shape["wide"]

    def per_device(amplitudes, partner, gate_block, slice_bits, bit_order):
        chosen = choose(partner, slice_bits)
        rows, cols = amplitudes.shape[1:]
        out_bits = gate_block.shape[0]
        low_rows = rows // wides
        block = chosen.shape[0]
        total = block * wides
        own = total // mesh.shape["narrow"]
        flat = out_bits * low_rows
        smem = pl.BlockSpec(memory_space=pltpu.SMEM)
        vmem = pl.BlockSpec(memory_space=pltpu.VMEM)
        dma = pltpu.SemaphoreType.DMA
        lines = wides // 2
        return pl.pallas_call(
            functools.partial(kernel, wides),
            out_shape=jax.ShapeDtypeStruct((out_bits, low_rows, own), F32),
            in_specs=[smem, smem, pl.BlockSpec(memory_space=pl.ANY), vmem],
            out_specs=vmem,
            scratch_shapes=[
                pltpu.VMEM((rows, cols), F32),
                pltpu.VMEM((wides, low_rows, cols), F32),
                pltpu.VMEM((wides, low_rows, cols), F32),
                pltpu.VMEM((out_bits, low_rows, cols), F32),
                pltpu.VMEM((flat, cols), BF16),
                pltpu.VMEM((flat, cols), BF16),
                pltpu.VMEM((wides, block, cols), F32),
                pltpu.VMEM((2, flat, own), F32),
                pltpu.VMEM((2, flat, own), F32),
                pltpu.VMEM((flat, own), F32),
                pltpu.VMEM((flat, own), F32),
                pltpu.VMEM((flat, own), F32),
                dma,
                dma((wides,)), dma((wides,)),
                *[dma((lines, HALVES))] * 5,
                dma((PIECES,)), dma((PIECES,)), dma, dma, dma((PIECES,)), dma((PIECES,)),
            ],
            compiler_params=pltpu.CompilerParams(
                collective_id=0, has_side_effects=True, vmem_limit_bytes=48 * 1024 * 1024),
        )(bit_order, gate_block, amplitudes[0], chosen)

    placed = (P("wide", None, "narrow"), P(None, "wide", "narrow"), P(), P(), P())
    return jax.shard_map(
        per_device, mesh=mesh, in_specs=placed, out_specs=P(None, "wide", "narrow"), check_vma=False
    )
```

time: 63.2 us -> 61.5 us (0.973)
  Pallas kernels: 61 us -> 59.4 us
    pallas_call x1, Pallas kernels: 58.5 us -> 56.9 us  [per_device(): pl.pallas_call(functools.partial(kernel, wides), out_shape=jax.ShapeDtype...]
where the time goes in v2:
time: 61.5 us; the launch traced here: 61.4 us
  Pallas kernels  59.4 us (97%)
  local copies, waits for them, and re-layouts  1.93 us (3%)
    pallas_call x1, Pallas kernels, per_device(): pl.pallas_call(functools.partial(kernel, wides), out_shape=jax.ShapeDtype...  56.9 us
    pallas_call x1, Pallas kernels, choose(): pl.pallas_call(slice_kernel, out_shape=jax.ShapeDtypeStruct((rows, cols),...  2.46 us
    unnamed x9, local copies, waits for them, and re-layouts  1.93 us

profile of v2, /device:TPU:1, one launch (start us, length us, event | category | flops | bytes accessed | tf_op | source)
XLA Modules:
  0.0 61.4 jit_solution(5578717716292248931)
XLA Ops:
  0.0 0.0 copy-start.3
  0.0 0.0 copy-start.2
  0.0 0.0 copy-start.1
  0.0 2.5 %shard_map.55.chosen_ref = f32[256,256]{1,0:T(8,128)} custom-call(s32[6]{0:T(128)} %bits_ref.1, f32[64,256,256]{2,1,0:T(8,128)} %partner_ref.1), custom_call_target="tpu_custom_call" | custom-call | tf_op jit(solution)/shard_map/pallas_call | solution.py:25
  2.5 0.0 copy-done.3
  2.5 0.0 copy-done.2
  2.5 0.0 copy-done.1
  2.5 0.0 copy-start
  2.5 0.9 %copy-done = f32[256,256]{1,0:T(8,128)S(1)} copy-done((f32[256,256]{1,0:T(8,128)S(1)}, f32[256,256]{1,0:T(8,128)}, u32[]{:S(2)}) %copy-start) | copy-done | bytes 262168
  3.5 56.9 %shard_map.56 = f32[8,64,512]{2,1,0:T(8,128)S(1)} custom-call(s32[9]{0:T(128)S(1)} %copy-done.3, f32[8,8]{1,0:T(8,128)S(1)} %copy-done.2, f32[512,256]{1,0:T(8,128)S(1)} %bitcast.1, f32[256,256]{1,0:T(8,128)S(1)} %copy-done), custom_call_target="tpu_custom_call" | custom-call | tf_op jit(solution)/shard_map/pallas_call | solution.py:276
  60.4 1.0 %copy.7 = f32[8,64,512]{2,1,0:T(8,128)} copy(f32[8,64,512]{2,1,0:T(8,128)S(1)} %shard_map.56) | data formatting | bytes 2097152
Async XLA Ops:
  0.0 2.5 %copy-start.3 = (s32[9]{0:T(128)S(1)}, s32[9]{0:T(128)}, u32[]{:S(2)}) copy-start(s32[9]{0:T(128)} %order_ref.1) | copy-start | bytes 112
  0.0 2.5 %copy-start.2 = (f32[8,8]{1,0:T(8,128)S(1)}, f32[8,8]{1,0:T(8,128)}, u32[]{:S(2)}) copy-start(f32[8,8]{1,0:T(8,128)} %gate_ref.1) | copy-start | bytes 772
  0.0 2.5 %copy-start.1 = (f32[1,512,256]{2,1,0:T(8,128)S(1)}, f32[1,512,256]{2,1,0:T(8,128)}, u32[]{:S(2)}) copy-start(f32[1,512,256]{2,1,0:T(8,128)} %param.5) | copy-start | bytes 1572868
  2.5 1.0 %copy-start = (f32[256,256]{1,0:T(8,128)S(1)}, f32[256,256]{1,0:T(8,128)}, u32[]{:S(2)}) copy-start(f32[256,256]{1,0:T(8,128)} %shard_map.55.chosen_ref) | copy-start | bytes 786436

commit v3 on v2

--- a/solution.py
+++ b/solution.py
@@ -26,7 +26,7 @@
         slice_kernel,
         out_shape=jax.ShapeDtypeStruct((rows, cols), F32),
         in_specs=[pl.BlockSpec(memory_space=pltpu.SMEM), pl.BlockSpec(memory_space=pl.ANY)],
-        out_specs=pl.BlockSpec(memory_space=pltpu.VMEM),
+        out_specs=pl.BlockSpec(memory_space=pl.ANY),
         scratch_shapes=[pltpu.SemaphoreType.DMA],
     )(slice_bits, partner)
 
@@ -40,13 +40,13 @@
     return lax.dot_general(a, b, (((1,), (1,)), ((), ())), preferred_element_type=F32)
 
 
-PIECES = 4
+PIECES = 2
 HALVES = 2
 
 
 def kernel(wides, order_ref, gate_ref, amp_hbm, chosen_ref, out_ref,
            amp_ref, send_a, recv_a, mixed, mix_hi, mix_lo, held, far_part, near_part,
-           core_far, core_near, x_in, amp_sem,
+           core_far, core_near, x_in, amp_sem, own_sem,
            a_send, a_recv, up_send, down_send, z_recv, y_send, y_recv,
            far_send, far_recv, near_send, near_recv, x_send, x_recv):
     me = lax.axis_index("wide")
@@ -72,6 +72,8 @@
     barrier = pltpu.get_barrier_semaphore()
     amp_copy = pltpu.make_async_copy(amp_hbm, amp_ref, amp_sem)
     amp_copy.start()
+    own_copy = pltpu.make_async_copy(chosen_ref, held.at[me], own_sem)
+    own_copy.start()
 
     @pl.loop(1, wides)
     def _(s):
@@ -79,7 +81,6 @@
                             device_id_type=pl.DeviceIdType.MESH)
     for peer in (core_peer, x_peer):
         pl.semaphore_signal(barrier, inc=1, device_id=peer, device_id_type=pl.DeviceIdType.MESH)
-    held[me] = chosen_ref[...]
 
     row_ids = lax.broadcasted_iota(jnp.int32, (rows, 128), 0)
     source = jnp.zeros((rows, 128), jnp.int32)
@@ -89,6 +90,7 @@
     onehot = jnp.concatenate(
         [jnp.where(lane + t * 128 == source, 1.0, 0.0).astype(BF16) for t in range(rows // 128)], axis=1)
     amp_copy.wait()
+    own_copy.wait()
     amp = amp_ref[...]
     a1 = amp.astype(BF16)
     rest = amp - a1.astype(F32)
@@ -160,44 +162,61 @@
                     down(z + d, p).start()
                 across(z + d, p).start()
 
-    def product(o, dst, role):
+    subs = far_part.shape[1]
+
+    def cross_wait(o):
         @pl.loop(0, zs_per)
         def _(i):
             for p in range(HALVES):
                 across_in(o * zs_per + i, p).wait_recv()
-        b = held[pl.ds(o * group, group)].reshape(wide_cols, cols)
+
+    def times(b):
         bh, bl = split2(b)
         mh, ml = mix_hi[...], mix_lo[...]
-        dst[role] = dot_nt(mh, bl) + dot_nt(ml, bh) + dot_nt(mh, bh)
+        return dot_nt(mh, bl) + dot_nt(ml, bh) + dot_nt(mh, bh)
+
+    def product(o, role):
+        cross_wait(o)
+        b = held[pl.ds(o * group, group)].reshape(wide_cols, cols)
+        near_part[role] = times(b)
 
     piece = flat // PIECES
 
     def part(p):
         return pl.ds(p * piece, piece)
 
-    def far_core(p):
-        return rc(far_part.at[1, part(p)], core_far.at[part(p)], far_send.at[p], far_recv.at[p], core_peer)
-
-    def over_x(p):
-        return rc(far_part.at[0, part(p)], x_in.at[part(p)], x_send.at[p], x_recv.at[p], x_peer)
+    def far_core(v, p):
+        return rc(far_part.at[1, v, part(p)], core_far.at[v, part(p)], far_send.at[v, p], far_recv.at[v, p], core_peer)
+
+    def over_x(v, p):
+        return rc(far_part.at[0, v, part(p)], x_in.at[v, part(p)], x_send.at[v, p], x_recv.at[v, p], x_peer)
 
     near_core = rc(near_part.at[1], core_near, near_send, near_recv, core_peer)
 
-    def remote_chunk(o):
+    def remote_part(o, turn):
         role = (o + c) % 2
-        product(o, far_part, role)
+        if subs == 1:
+            v = 0
+            cross_wait(o)
+            b = held[pl.ds(o * group, group)].reshape(wide_cols, cols)
+        else:
+            v = (y + turn) % 2
+            if turn == 1:
+                cross_wait(o)
+            b = held[o * 2 + v]
+        far_part[role, v] = times(b)
 
         @pl.when(role == 1)
         def _():
             for p in range(PIECES):
-                far_core(p).start()
+                far_core(v, p).start()
 
         @pl.when(role == 0)
         def _():
             for p in range(PIECES):
-                far_core(p).wait_recv()
-                far_part[0, part(p)] = far_part[0, part(p)] + core_far[part(p)]
-                over_x(p).start()
+                far_core(v, p).wait_recv()
+                far_part[0, v, part(p)] = far_part[0, v, part(p)] + core_far[v, part(p)]
+                over_x(v, p).start()
 
     here = z // zs_per
     remote_low = (1 - x) * 2
@@ -221,24 +240,32 @@
     mix_hi[...] = hi
     mix_lo[...] = lo
 
-    remote_chunk(first)
+    remote_part(first, 0)
     for d in range(last_near + 1, lines):
         line_step(d)
-    remote_chunk(second)
-    product(x * 2 + 1 - c, near_part, 1)
+    for turn in range(1, subs):
+        remote_part(first, turn)
+    for turn in range(subs):
+        remote_part(second, turn)
+    product(x * 2 + 1 - c, 1)
     near_core.start()
-    product(nar, near_part, 0)
+    product(nar, 0)
     near_core.wait_recv()
     near_part[0] = near_part[0] + core_near[...]
-    for p in range(PIECES):
-        over_x(p).wait_recv()
-        qs = out_bits // PIECES
-        out_ref[p * qs:(p + 1) * qs] = (near_part[0, part(p)] + x_in[part(p)]).reshape(qs, low_rows, wide_cols)
+    qs = out_bits // PIECES
+    width = wide_cols // subs
+    for v in range(subs):
+        for p in range(PIECES):
+            over_x(v, p).wait_recv()
+            out_ref[p * qs:(p + 1) * qs, :, v * width:(v + 1) * width] = (
+                near_part[0, part(p), v * width:(v + 1) * width] + x_in[v, part(p)]
+            ).reshape(qs, low_rows, width)
 
     near_core.wait_send()
-    for p in range(PIECES):
-        far_core(p).wait_send()
-        over_x(p).wait_send()
+    for v in range(subs):
+        for p in range(PIECES):
+            far_core(v, p).wait_send()
+            over_x(v, p).wait_send()
 
     @pl.loop(1, wides)
     def _(s):
@@ -273,10 +300,11 @@
         vmem = pl.BlockSpec(memory_space=pltpu.VMEM)
         dma = pltpu.SemaphoreType.DMA
         lines = wides // 2
+        subs = 2 if own == 2 * block else 1
         return pl.pallas_call(
             functools.partial(kernel, wides),
             out_shape=jax.ShapeDtypeStruct((out_bits, low_rows, own), F32),
-            in_specs=[smem, smem, pl.BlockSpec(memory_space=pl.ANY), vmem],
+            in_specs=[smem, smem, pl.BlockSpec(memory_space=pl.ANY), pl.BlockSpec(memory_space=pl.ANY)],
             out_specs=vmem,
             scratch_shapes=[
                 pltpu.VMEM((rows, cols), F32),
@@ -286,18 +314,18 @@
                 pltpu.VMEM((flat, cols), BF16),
                 pltpu.VMEM((flat, cols), BF16),
                 pltpu.VMEM((wides, block, cols), F32),
+                pltpu.VMEM((2, subs, flat, own // subs), F32),
                 pltpu.VMEM((2, flat, own), F32),
-                pltpu.VMEM((2, flat, own), F32),
+                pltpu.VMEM((subs, flat, own // subs), F32),
                 pltpu.VMEM((flat, own), F32),
-                pltpu.VMEM((flat, own), F32),
-                pltpu.VMEM((flat, own), F32),
-                dma,
+                pltpu.VMEM((subs, flat, own // subs), F32),
+                dma, dma,
                 dma((wides,)), dma((wides,)),
                 *[dma((lines, HALVES))] * 5,
-                dma((PIECES,)), dma((PIECES,)), dma, dma, dma((PIECES,)), dma((PIECES,)),
+                dma((subs, PIECES)), dma((subs, PIECES)), dma, dma, dma((subs, PIECES)), dma((subs, PIECES)),
             ],
             compiler_params=pltpu.CompilerParams(
-                collective_id=0, has_side_effects=True, vmem_limit_bytes=48 * 1024 * 1024),
+                collective_id=0, has_side_effects=True, vmem_limit_bytes=60 * 1024 * 1024),
         )(bit_order, gate_block, amplitudes[0], chosen)
 
     placed = (P("wide", None, "narrow"), P(None, "wide", "narrow"), P(), P(), P())

time: 61.5 us -> 69.2 us (1.13)
  Pallas kernels: 59.4 us -> 66.3 us
    pallas_call x1, Pallas kernels: 2.46 us -> 9.72 us  [choose(): pl.pallas_call(slice_kernel, out_shape=jax.ShapeDtypeStruct((rows, cols),...]
    unnamed x9 -> x1, local copies, waits for them, and re-layouts: 1.93 us -> 2.26 us
where the time goes in v3:
time: 69.2 us; the launch traced here: 68.6 us
  Pallas kernels  66.3 us (96%)
  local copies, waits for them, and re-layouts  2.26 us (3%)
    pallas_call x1, Pallas kernels, per_device(): pl.pallas_call(functools.partial(kernel, wides), out_shape=jax.ShapeDtype...  56.6 us
    pallas_call x1, Pallas kernels, choose(): pl.pallas_call(slice_kernel, out_shape=jax.ShapeDtypeStruct((rows, cols),...  9.72 us
    unnamed x1, local copies, waits for them, and re-layouts  2.26 us

profile of v3, /device:TPU:1, one launch (start us, length us, event | category | flops | bytes accessed | tf_op | source)
XLA Modules:
  0.0 68.6 jit_solution(14237160689014753451)
XLA Ops:
  0.0 9.7 %shard_map.55.chosen_ref = f32[256,256]{1,0:T(8,128)} custom-call(s32[6]{0:T(128)} %bits_ref.1, f32[64,256,256]{2,1,0:T(8,128)} %partner_ref.1), custom_call_target="tpu_custom_call" | custom-call | tf_op jit(solution)/shard_map/pallas_call | solution.py:25
  9.7 56.6 %shard_map.56 = f32[8,64,512]{2,1,0:T(8,128)} custom-call(s32[9]{0:T(128)} %order_ref.1, f32[8,8]{1,0:T(8,128)} %gate_ref.1, f32[512,256]{1,0:T(8,128)} %bitcast.1, f32[256,256]{1,0:T(8,128)} %shard_map.55.chosen_ref), custom_call_target="tpu_custom_call" | custom-call | tf_op jit(solution)/shard_map/pallas_call | solution.py:304
  66.3 2.3 %copy.7 = f32[8,64,512]{2,1,0:T(8,128)} copy(f32[8,64,512]{2,1,0:T(8,128)} %shard_map.56) | data formatting | bytes 2097152

commit v4 on v3

--- a/solution.py
+++ b/solution.py
@@ -24,9 +24,9 @@
     _, rows, cols = partner.shape
     return pl.pallas_call(
         slice_kernel,
-        out_shape=jax.ShapeDtypeStruct((rows, cols), F32),
+        out_shape=pltpu.VMEM((rows, cols), F32),
         in_specs=[pl.BlockSpec(memory_space=pltpu.SMEM), pl.BlockSpec(memory_space=pl.ANY)],
-        out_specs=pl.BlockSpec(memory_space=pl.ANY),
+        out_specs=pl.BlockSpec(memory_space=pltpu.VMEM),
         scratch_shapes=[pltpu.SemaphoreType.DMA],
     )(slice_bits, partner)
 
@@ -325,7 +325,7 @@
                 dma((subs, PIECES)), dma((subs, PIECES)), dma, dma, dma((subs, PIECES)), dma((subs, PIECES)),
             ],
             compiler_params=pltpu.CompilerParams(
-                collective_id=0, has_side_effects=True, vmem_limit_bytes=60 * 1024 * 1024),
+                collective_id=0, has_side_effects=True, vmem_limit_bytes=48 * 1024 * 1024),
         )(bit_order, gate_block, amplitudes[0], chosen)
 
     placed = (P("wide", None, "narrow"), P(None, "wide", "narrow"), P(), P(), P())

time: 69.2 us -> 58.9 us (0.85)
  Pallas kernels: 66.3 us -> 57.3 us
  local copies, waits for them, and re-layouts: 2.26 us -> 0.98 us
    pallas_call x1, Pallas kernels: 9.72 us -> 1.76 us  [choose(): pl.pallas_call(slice_kernel, out_shape=pltpu.VMEM((rows, cols), F32), in_...]
    unnamed x1 -> x7, local copies, waits for them, and re-layouts: 2.26 us -> 0.98 us
    pallas_call x1, Pallas kernels: 56.6 us -> 55.5 us  [per_device(): pl.pallas_call(functools.partial(kernel, wides), out_shape=jax.ShapeDtype...]
where the time goes in v4:
time: 58.9 us; the launch traced here: 58.3 us
  Pallas kernels  57.3 us (97%)
  local copies, waits for them, and re-layouts  0.98 us (2%)
    pallas_call x1, Pallas kernels, per_device(): pl.pallas_call(functools.partial(kernel, wides), out_shape=jax.ShapeDtype...  55.5 us
    pallas_call x1, Pallas kernels, choose(): pl.pallas_call(slice_kernel, out_shape=pltpu.VMEM((rows, cols), F32), in_...  1.76 us

profile of v4, /device:TPU:1, one launch (start us, length us, event | category | flops | bytes accessed | tf_op | source)
XLA Modules:
  0.0 58.3 jit_solution(1362012543072904825)
XLA Ops:
  0.0 0.0 copy-start.2
  0.0 0.0 copy-start.1
  0.0 0.0 copy-start
  0.0 1.8 %shard_map.55.chosen_ref = f32[256,256]{1,0:T(8,128)S(1)} custom-call(s32[6]{0:T(128)} %bits_ref.1, f32[64,256,256]{2,1,0:T(8,128)} %partner_ref.1), custom_call_target="tpu_custom_call" | custom-call | tf_op jit(solution)/shard_map/pallas_call | solution.py:25
  1.8 0.0 copy-done.2
  1.8 0.0 copy-done.1
  1.8 0.0 copy-done
  1.8 55.5 %shard_map.56 = f32[8,64,512]{2,1,0:T(8,128)S(1)} custom-call(s32[9]{0:T(128)S(1)} %copy-done.2, f32[8,8]{1,0:T(8,128)S(1)} %copy-done.1, f32[512,256]{1,0:T(8,128)S(1)} %bitcast.1, f32[256,256]{1,0:T(8,128)S(1)} %shard_map.55.chosen_ref), custom_call_target="tpu_custom_call" | custom-call | tf_op jit(solution)/shard_map/pallas_call | solution.py:304
  57.4 1.0 %copy.7 = f32[8,64,512]{2,1,0:T(8,128)} copy(f32[8,64,512]{2,1,0:T(8,128)S(1)} %shard_map.56) | data formatting | bytes 2097152
Async XLA Ops:
  0.0 1.8 %copy-start.2 = (s32[9]{0:T(128)S(1)}, s32[9]{0:T(128)}, u32[]{:S(2)}) copy-start(s32[9]{0:T(128)} %order_ref.1) | copy-start | bytes 112
  0.0 1.8 %copy-start.1 = (f32[8,8]{1,0:T(8,128)S(1)}, f32[8,8]{1,0:T(8,128)}, u32[]{:S(2)}) copy-start(f32[8,8]{1,0:T(8,128)} %gate_ref.1) | copy-start | bytes 772
  0.0 1.8 %copy-start = (f32[1,512,256]{2,1,0:T(8,128)S(1)}, f32[1,512,256]{2,1,0:T(8,128)}, u32[]{:S(2)}) copy-start(f32[1,512,256]{2,1,0:T(8,128)} %param.5) | copy-start | bytes 1572868

commit v5 on v4

--- a/solution.py
+++ b/solution.py
@@ -223,8 +223,7 @@
     first = jnp.where(here > remote_low, remote_low + 1, remote_low)
     second = remote_low * 2 + 1 - first
     last_near = max(3 * zs_per - 1, 1)
-    for d in range(1, last_near + 1):
-        line_step(d)
+    line_step(1)
 
     @pl.loop(1, wides)
     def _(s):
@@ -240,6 +239,8 @@
     mix_hi[...] = hi
     mix_lo[...] = lo
 
+    for d in range(2, last_near + 1):
+        line_step(d)
     remote_part(first, 0)
     for d in range(last_near + 1, lines):
         line_step(d)

time: 58.9 us -> 58.5 us (level)
  no operation moved by 1% of the time
where the time goes in v5:
time: 58.5 us; the launch traced here: 58.3 us
  Pallas kernels  57.3 us (98%)
  local copies, waits for them, and re-layouts  0.98 us (2%)
    pallas_call x1, Pallas kernels, per_device(): pl.pallas_call(functools.partial(kernel, wides), out_shape=jax.ShapeDtype...  55.5 us
    pallas_call x1, Pallas kernels, choose(): pl.pallas_call(slice_kernel, out_shape=pltpu.VMEM((rows, cols), F32), in_...  1.76 us

profile of v5, /device:TPU:1, one launch (start us, length us, event | category | flops | bytes accessed | tf_op | source)
XLA Modules:
  0.0 58.3 jit_solution(6128619428886825526)
XLA Ops:
  0.0 0.0 copy-start.2
  0.0 0.0 copy-start.1
  0.0 0.0 copy-start
  0.0 1.8 %shard_map.55.chosen_ref = f32[256,256]{1,0:T(8,128)S(1)} custom-call(s32[6]{0:T(128)} %bits_ref.1, f32[64,256,256]{2,1,0:T(8,128)} %partner_ref.1), custom_call_target="tpu_custom_call" | custom-call | tf_op jit(solution)/shard_map/pallas_call | solution.py:25
  1.8 0.0 copy-done.2
  1.8 0.0 copy-done.1
  1.8 0.0 copy-done
  1.8 55.5 %shard_map.56 = f32[8,64,512]{2,1,0:T(8,128)S(1)} custom-call(s32[9]{0:T(128)S(1)} %copy-done.2, f32[8,8]{1,0:T(8,128)S(1)} %copy-done.1, f32[512,256]{1,0:T(8,128)S(1)} %bitcast.1, f32[256,256]{1,0:T(8,128)S(1)} %shard_map.55.chosen_ref), custom_call_target="tpu_custom_call" | custom-call | tf_op jit(solution)/shard_map/pallas_call | solution.py:305
  57.4 1.0 %copy.7 = f32[8,64,512]{2,1,0:T(8,128)} copy(f32[8,64,512]{2,1,0:T(8,128)S(1)} %shard_map.56) | data formatting | bytes 2097152
Async XLA Ops:
  0.0 1.8 %copy-start.2 = (s32[9]{0:T(128)S(1)}, s32[9]{0:T(128)}, u32[]{:S(2)}) copy-start(s32[9]{0:T(128)} %order_ref.1) | copy-start | bytes 112
  0.0 1.8 %copy-start.1 = (f32[8,8]{1,0:T(8,128)S(1)}, f32[8,8]{1,0:T(8,128)}, u32[]{:S(2)}) copy-start(f32[8,8]{1,0:T(8,128)} %gate_ref.1) | copy-start | bytes 772
  0.0 1.8 %copy-start = (f32[1,512,256]{2,1,0:T(8,128)S(1)}, f32[1,512,256]{2,1,0:T(8,128)}, u32[]{:S(2)}) copy-start(f32[1,512,256]{2,1,0:T(8,128)} %param.5) | copy-start | bytes 1572868
